TPU v7x, 32 devices: a whole 2x2x4 slice. The times are simulated.
32 devices in a mesh: tm: 4 (over y, x), space: 8 (over z, core).
Axes of the slice: x: 2, y: 2, z: 4, core: 2. Of those that a mesh axis runs over, the one named last changes fastest.
Arguments:
- vectors: float32 [4, 2, 3, 64, 2048], P('tm', None, None, None, 'space'), may hold values from -6 to 6
- perambulators: float32 [4, 16, 2, 4096], P('tm'), may hold values from -0.75 to 0.75
- shift_steps: int32 [4], P('tm'), may hold values from 1 to 3, as said below
- spin_choice: int32 [4, 3], replicated, may hold values from 0 to 15
Outputs:
- elementals: float32 [4, 64, 2, 4096], P('tm', 'space')
- correlator: float32 [4, 4, 2], P('tm')
Inputs may be any that keep to these rules, and one draw needn't show every extreme that they name: `shift_steps`: every distance from 1 to 3 is taken by at least one source timeslice. `spin_choice`: each entry is alpha 4 + beta for a pair of spin indices.
All inputs are finite; a program needn't handle non-finite values.
Results may differ from a plain program's by a relative error of at most 0.0003.
Values sent between devices are 32-bit elements; how exact they have to be, the bound alone decides.
A program may use at most 64 MiB of HBM per device.

v0:
```python
import math
import jax
import jax.numpy as jnp
from jax import lax
from jax.sharding import PartitionSpec as P

exact_mode = lax.Precision.HIGHEST


def complex_product(left_re, left_im, right_re, right_im):
    return (left_re * right_re - left_im * right_im, left_re * right_im + left_im * right_re)


def rotate(values, places):
    return jnp.concatenate([values[places:], values[:places]], axis=0)


def contract_first(left, right):
    return lax.dot_general(left, right, (((0,), (0,)), ((), ())), precision=exact_mode)


def inner_rows(left, right):
    return lax.dot_general(left, right, (((1,), (1,)), ((), ())), precision=exact_mode)


def complex_einsum(form, left, right):
    first = jnp.einsum(form, left[0], right[0], precision=exact_mode) - jnp.einsum(
        form, left[1], right[1], precision=exact_mode
    )
    second = jnp.einsum(form, left[0], right[1], precision=exact_mode) + jnp.einsum(
        form, left[1], right[0], precision=exact_mode
    )
    return (first, second)


def elemental_rows(vec_re, vec_im, lead_re, lead_im, first_row, row_count, factor):
    sites = vec_re.shape[1]
    nvec = vec_re.shape[2]
    block = math.gcd(row_count, 4)

    def one_block(index):
        offset = first_row + index * block
        part_re = lax.dynamic_slice_in_dim(vec_re, offset, block, 2)[:, :, :, None]
        part_im = lax.dynamic_slice_in_dim(vec_im, offset, block, 2)[:, :, :, None]
        full_re = vec_re[:, :, None, :]
        full_im = vec_im[:, :, None, :]
        one_re, one_im = complex_product(
            rotate(part_re, 1), rotate(part_im, 1), rotate(full_re, 2), rotate(full_im, 2)
        )
        two_re, two_im = complex_product(
            rotate(part_re, 2), rotate(part_im, 2), rotate(full_re, 1), rotate(full_im, 1)
        )
        cross_re = (one_re - two_re).reshape(3 * sites, block * nvec)
        cross_im = (one_im - two_im).reshape(3 * sites, block * nvec)
        out_re = contract_first(lead_re, cross_re) - contract_first(lead_im, cross_im)
        out_im = contract_first(lead_re, cross_im) + contract_first(lead_im, cross_re)
        stacked = jnp.stack([out_re, out_im], 0).reshape(2, nvec, block, nvec)
        return jnp.transpose(stacked, (2, 0, 1, 3)).reshape(block, 2, nvec * nvec) * factor

    result = lax.map(one_block, jnp.arange(row_count // block, dtype=jnp.int32))
    return result.reshape(row_count, 2, nvec * nvec)


def transform_rows(own, mats, nvec):
    combos = mats.shape[0]
    row_count = own.shape[0]
    elem = (own[:, 0].reshape(row_count, nvec, nvec), own[:, 1].reshape(row_count, nvec, nvec))
    first_mat = (
        mats[:, 0, 0].reshape(combos, nvec, nvec),
        mats[:, 0, 1].reshape(combos, nvec, nvec),
    )
    third_mat = (
        mats[:, 2, 0].reshape(combos, nvec, nvec),
        mats[:, 2, 1].reshape(combos, nvec, nvec),
    )
    half = complex_einsum("jik,slk->sjil", elem, third_mat)
    done = complex_einsum("smi,sjil->sjml", first_mat, half)
    return (
        done[0].reshape(combos * row_count, nvec * nvec),
        done[1].reshape(combos * row_count, nvec * nvec),
    )


def pair_sum(sink_rows, trans_re, trans_im, mid_re, mid_im):
    combos = mid_re.shape[0]
    sink_count = sink_rows.shape[0]
    own_count = mid_re.shape[2]
    sink_re = sink_rows[:, 0]
    sink_im = sink_rows[:, 1]
    inner_re = (inner_rows(sink_re, trans_re) + inner_rows(sink_im, trans_im)).reshape(
        sink_count, combos, own_count
    )
    inner_im = (inner_rows(sink_re, trans_im) - inner_rows(sink_im, trans_re)).reshape(
        sink_count, combos, own_count
    )
    total_re = jnp.einsum("srj,rsj->s", mid_re, inner_re, precision=exact_mode) - jnp.einsum(
        "srj,rsj->s", mid_im, inner_im, precision=exact_mode
    )
    total_im = jnp.einsum("srj,rsj->s", mid_re, inner_im, precision=exact_mode) + jnp.einsum(
        "srj,rsj->s", mid_im, inner_re, precision=exact_mode
    )
    return jnp.stack([total_re, total_im], -1)


def shards(vectors, perambulators, shift_steps, spin_choice):
    local_vec = vectors[0]
    nvec = local_vec.shape[2]
    sites = local_vec.shape[3]
    space_count = lax.axis_size("space")
    time_count = lax.axis_size("tm")
    vec_re = jnp.transpose(local_vec[0], (0, 2, 1))
    vec_im = jnp.transpose(local_vec[1], (0, 2, 1))
    lead_re = vec_re.reshape(3 * sites, nvec)
    lead_im = vec_im.reshape(3 * sites, nvec)
    factor = 1.0 / math.sqrt(24.0 * sites * space_count)
    corr_factor = 0.25 / (nvec * math.sqrt(nvec))
    own_count = nvec // space_count
    own_first = lax.axis_index("space") * own_count
    summed = lax.psum(elemental_rows(vec_re, vec_im, lead_re, lead_im, 0, nvec, factor), "space")
    own = lax.dynamic_slice_in_dim(summed, own_first, own_count, 0)
    every_time = lax.all_gather(own[None], "tm", axis=0, tiled=True)
    target = (lax.axis_index("tm") + shift_steps[0]) % time_count
    sink = lax.dynamic_index_in_dim(every_time, target, 0, keepdims=False)
    combos = spin_choice.shape[0]
    spin_pairs = perambulators.shape[1]
    one_hot = (
        spin_choice[:, :, None] == jnp.arange(spin_pairs, dtype=jnp.int32)[None, None, :]
    ).astype(jnp.float32)
    mats = jnp.einsum("sqm,mcf->sqcf", one_hot, perambulators[0], precision=exact_mode)
    trans_re, trans_im = transform_rows(own, mats, nvec)
    mid_re = lax.dynamic_slice_in_dim(
        mats[:, 1, 0].reshape(combos, nvec, nvec), own_first, own_count, 2
    )
    mid_im = lax.dynamic_slice_in_dim(
        mats[:, 1, 1].reshape(combos, nvec, nvec), own_first, own_count, 2
    )
    sink_rows = lax.all_gather(sink, "space", axis=0, tiled=True)
    partial_corr = pair_sum(sink_rows, trans_re, trans_im, mid_re, mid_im)
    correlator = lax.psum(partial_corr, "space") * corr_factor
    return (own[None], correlator[None])


def solution(mesh):
    placed = (P("tm", None, None, None, "space"), P("tm", None, None, None), P("tm"), P())
    return jax.shard_map(
        shards,
        mesh=mesh,
        in_specs=placed,
        out_specs=(P("tm", "space", None, None), P("tm", None, None)),
        check_vma=False,
    )
```

profile of v0, /device:TPU:0, one launch (start us, length us, event | category | flops | bytes accessed | tf_op | source)
XLA Modules:
  0.0 342.0 jit_solution(15728689861665589250)
XLA Ops:
  7.2 1.0 fusion.30
  8.3 1.1 copy_bitcast_fusion
  9.3 1.1 slice_bitcast_fusion.7
  10.5 1.1 slice_bitcast_fusion.11
  11.6 1.1 slice_bitcast_fusion.6
  12.8 1.1 slice_bitcast_fusion.10
  13.9 1.1 copy.20
  15.0 1.1 copy.21
  16.7 163.7 %while.11 = (s32[]{:T(128)}, f32[16,4,2,4096]{3,2,1,0:T(2,128)}, s32[16]{0:T(128)S(1)}, f32[3,256,64]{1,0,2:T(4,128)}, f32[3,256,1,64]{1,0,3,2:T(4,128)S(1)}, /*...) while((s32[]{:T(128)}, f32[16,4,2,4096]{3,2,1,0:T(2,128)}, ...), condition=%wide.region_1.2_spmd, body=%wide.region_0.1_spmd.sunk | while | flops 606842880 | bytes 11387647 | solution.py:60
  21.9 1.4 fusion.77
  32.1 1.4 fusion.77
  42.4 1.4 fusion.77
  52.6 1.4 fusion.77
  62.8 1.4 fusion.77
  73.1 1.4 fusion.77
  83.3 1.4 fusion.77
  93.5 1.4 fusion.77
  103.8 1.4 fusion.77
  114.0 1.4 fusion.77
  124.2 1.4 fusion.77
  134.4 1.4 fusion.77
  144.7 1.4 fusion.77
  154.9 1.4 fusion.77
  165.1 1.4 fusion.77
  175.3 1.4 fusion.77
  180.4 4.1 %copy.22 = f32[64,2,4096]{2,0,1:T(8,128)} copy(f32[64,2,4096]{2,1,0:T(2,128)} %bitcast.264) | data formatting | bytes 4194304 | tf_op jit(solution)/shard_map/reshape | solution.py:61
  184.6 67.9 %all-reduce.2.cloned.1.call-done = f32[64,2,4096]{2,0,1:T(8,128)} async-done(((f32[64,2,4096]{2,0,1:T(8,128)}), f32[64,2,4096]{2,0,1:T(8,128)}) %all-reduce.2.cloned.1.call-update) | async-done | bytes 2097168 | tf_op jit(solution)/shard_map/psum | solution.py:119
  252.5 1.7 constant_dynamic-slice_fusion.3
  255.9 25.2 %all-gather.5.cloned.1.call-done = f32[32,2,4096]{2,0,1:T(8,128)} async-done(((f32[8,2,4096]{2,0,1:T(8,128)}), f32[32,2,4096]{2,0,1:T(8,128)}) %all-gather.5.cloned.1.call-update) | async-done | bytes 1048592 | tf_op jit(solution)/shard_map/all_gather | solution.py:121
  281.1 1.7 constant_dynamic-slice_fusion.2
  283.9 1.0 constant_dynamic-slice_fusion
  285.1 1.0 fusion.20
  286.1 1.0 fusion.24
  287.1 1.0 fusion.5
  288.1 1.0 fusion.16
  289.2 1.0 fusion.6
  290.2 1.0 fusion.3
  291.2 1.3 copy.27
  292.6 1.6 reshape.145
  294.1 1.0 fusion.18
  295.2 1.0 fusion.4
  296.2 1.3 copy.26
  297.5 1.6 reshape.144
  299.1 12.9 %all-gather.7.cloned.1.call-done = f32[1,64,2,4096]{3,1,0,2:T(8,128)} async-done(((f32[1,8,2,4096]{3,1,0,2:T(8,128)}), f32[1,64,2,4096]{3,1,0,2:T(8,128)}) %all-gather.7.cloned.1.call-update) | async-done | bytes 2097168 | tf_op jit(solution)/shard_map/all_gather | solution.py:137
  312.1 2.3 fusion.9
  314.4 2.2 fusion.10
  317.6 1.1 multiply_reduce_fusion.2
  319.6 15.2 %psum.15 = f32[4,2]{0,1:T(2,128)S(1)} all-reduce(f32[4,2]{0,1:T(2,128)S(1)} %pad_maximum_fusion.4), channel_id=1, replica_groups=mesh['tm'=4,'space'=8] {'space'}, use_global_device_ids=true, to_apply=%region_3.4 | all-reduce | flops 8 | bytes 64 | tf_op jit(solution)/shard_map/psum | solution.py:139
  (344 shorter events, 133.5 us)
Async XLA Ops:
  7.2 245.4 %all-reduce.2.cloned.1.call-start = ((), (), s32[]{:S(2)}) async-start(), calls=%async_computation | async-start | bytes 4194304 | tf_op jit(solution)/shard_map/psum | solution.py:119
  184.5 70.6 %copy-start.3 = (s32[4,3]{1,0:T(4,128)S(1)}, s32[4,3]{1,0:T(4,128)}, u32[]{:S(2)}) copy-start(s32[4,3]{1,0:T(4,128)} %param.9) | copy-start | bytes 148
  184.5 70.7 %copy-start.2 = (f32[1,16,2,4096]{3,2,1,0:T(2,128)S(1)}, f32[1,16,2,4096]{3,2,1,0:T(2,128)}, u32[]{:S(2)}) copy-start(f32[1,16,2,4096]{3,2,1,0:T(2,128)} %param.7) | copy-start | bytes 1572868
  184.5 96.6 %all-gather.5.cloned.1.call-start = ((), (), s32[]{:S(2)}) async-start(), calls=%async_computation.1 | async-start | bytes 1310720 | tf_op jit(solution)/shard_map/all_gather | solution.py:121
  254.2 57.9 %all-gather.7.cloned.1.call-start = ((), (), s32[]{:S(2)}) async-start(), calls=%async_computation.2 | async-start | bytes 2359296 | tf_op jit(solution)/shard_map/all_gather | solution.py:137
  312.1 4.5 %copy-start = (f32[1,64,2,4096]{3,1,0,2:T(8,128)S(1)}, f32[1,64,2,4096]{3,1,0,2:T(8,128)}, u32[]{:S(2)}) copy-start(f32[1,64,2,4096]{3,1,0,2:T(8,128)} %all-gather.7.cloned.1.call-done) | copy-start | bytes 6291460
  314.4 4.3 %copy-start.1 = (f32[8,2,4096]{2,0,1:T(8,128)S(1)}, f32[8,2,4096]{2,0,1:T(8,128)}, u32[]{:S(2)}) copy-start(f32[8,2,4096]{2,0,1:T(8,128)} %constant_dynamic-slice_fusion.3) | copy-start | bytes 786436
Sparse Core Ops, SparseCore 0:
  184.6 67.8 all-reduce.1
  254.9 26.0 all-gather.4
  282.9 29.1 all-gather.6
where the time goes:
time: 347 us; the launch traced here: 342 us
  waiting for transfers between devices  106 us (31%)
  local copies, waits for them, and re-layouts  97.5 us (28%)
  matrix products  76.3 us (22%)
  other arithmetic  18.9 us (5%)
  blocking collectives  15.2 us (4%)
  between operations  14.7 us (4%)
  loops' own time  12.9 us (4%)
    psum x1, waiting for transfers between devices, shards(): lax.psum(elemental_rows(vec_re, vec_im, lead_re, lead_im, 0, nvec, factor...  67.9 us
    dot_general x64, matrix products, contract_first(): lax.dot_general(left, right, (((0,), (0,)), ((), ())), precision=exact_mode)  60.9 us
    slice x36, local copies, waits for them, and re-layouts, rotate(): return jnp.concatenate([values[places:], values[:places]], axis=0)  30.9 us
    all_gather x1, waiting for transfers between devices, shards(): every_time = lax.all_gather(own[None], 'tm', axis=0, tiled=True)  25.2 us
    another operation x32, local copies, waits for them, and re-layouts, one_block(): stacked = jnp.stack([out_re, out_im], 0).reshape(2, nvec, block, nvec)  17 us
    sub x16, other arithmetic, one_block(): cross_re = (one_re - two_re).reshape(3 * sites, block * nvec)  15.5 us
    psum x1, blocking collectives, shards(): correlator = lax.psum(partial_corr, 'space') * corr_factor  15.2 us
    all_gather x1, waiting for transfers between devices, shards(): sink_rows = lax.all_gather(sink, 'space', axis=0, tiled=True)  12.9 us
  transfers between devices with their start and end apart: 3, of which 3 were waited for; matrix products, arithmetic and copies ran while one was open for 5% of the time, Pallas kernels for 0%

commit v1 on v0

--- a/solution.py
+++ b/solution.py
@@ -1,3 +1,4 @@
+import functools
 import math
 import jax
 import jax.numpy as jnp
@@ -5,6 +6,14 @@
 from jax.sharding import PartitionSpec as P
 
 exact_mode = lax.Precision.HIGHEST
+
+
+def cut_positions(z_in, mesh_ax):
+    t_next = lax.all_gather(z_in, mesh_ax).sum(axis=0)
+    return t_next
+
+
+return_all_the_words = functools.partial(cut_positions, mesh_ax="space")
 
 
 def complex_product(left_re, left_im, right_re, right_im):
@@ -116,7 +125,7 @@
     corr_factor = 0.25 / (nvec * math.sqrt(nvec))
     own_count = nvec // space_count
     own_first = lax.axis_index("space") * own_count
-    summed = lax.psum(elemental_rows(vec_re, vec_im, lead_re, lead_im, 0, nvec, factor), "space")
+    summed = return_all_the_words(elemental_rows(vec_re, vec_im, lead_re, lead_im, 0, nvec, factor))
     own = lax.dynamic_slice_in_dim(summed, own_first, own_count, 0)
     every_time = lax.all_gather(own[None], "tm", axis=0, tiled=True)
     target = (lax.axis_index("tm") + shift_steps[0]) % time_count

time: 347 us -> 438 us (1.26)
  waiting for transfers between devices: 106 us -> 190 us
  other arithmetic: 18.9 us -> 26.3 us
    all_gather x0 -> x1, waiting for transfers between devices: none -> 154 us  [cut_positions(): t_next = lax.all_gather(z_in, mesh_ax).sum(axis=0)]
    psum x1 -> x0, waiting for transfers between devices: 67.9 us -> none  [shards(): lax.psum(elemental_rows(vec_re, vec_im, lead_re, lead_im, 0, nvec, factor...]
    reduce_sum x0 -> x1, other arithmetic: none -> 7.37 us  [cut_positions(): t_next = lax.all_gather(z_in, mesh_ax).sum(axis=0)]
    slice x0 -> x1, local copies, waits for them, and re-layouts: none -> 4.64 us  [pair_sum(): sink_im = sink_rows[:, 1]]
  transfers between devices with their start and end apart: 3 -> 3, of which waited for: 3 -> 3; matrix products, arithmetic and copies ran while one was open for 5% -> 4% of each run, Pallas kernels for 0% -> 0%
where the time goes in v1:
time: 438 us; the launch traced here: 434 us
  waiting for transfers between devices  190 us (43%)
  local copies, waits for them, and re-layouts  99.8 us (23%)
  matrix products  76.2 us (17%)
  other arithmetic  26.3 us (6%)
  blocking collectives  15.3 us (3%)
  between operations  14.7 us (3%)
  loops' own time  11.8 us (3%)
    all_gather x1, waiting for transfers between devices, cut_positions(): t_next = lax.all_gather(z_in, mesh_ax).sum(axis=0)  154 us
    dot_general x64, matrix products, contract_first(): lax.dot_general(left, right, (((0,), (0,)), ((), ())), precision=exact_mode)  60.9 us
    slice x36, local copies, waits for them, and re-layouts, rotate(): return jnp.concatenate([values[places:], values[:places]], axis=0)  30.9 us
    all_gather x1, waiting for transfers between devices, shards(): every_time = lax.all_gather(own[None], 'tm', axis=0, tiled=True)  23.8 us
    another operation x32, local copies, waits for them, and re-layouts, one_block(): stacked = jnp.stack([out_re, out_im], 0).reshape(2, nvec, block, nvec)  17 us
    sub x16, other arithmetic, one_block(): cross_re = (one_re - two_re).reshape(3 * sites, block * nvec)  15.5 us
    psum x1, blocking collectives, shards(): correlator = lax.psum(partial_corr, 'space') * corr_factor  15.3 us
    all_gather x1, waiting for transfers between devices, shards(): sink_rows = lax.all_gather(sink, 'space', axis=0, tiled=True)  11.9 us
  transfers between devices with their start and end apart: 3, of which 3 were waited for; matrix products, arithmetic and copies ran while one was open for 4% of the time, Pallas kernels for 0%

profile of v1, /device:TPU:0, one launch (start us, length us, event | category | flops | bytes accessed | tf_op | source)
XLA Modules:
  0.0 434.0 jit_solution(424042090725161822)
XLA Ops:
  7.2 1.0 fusion.39
  8.3 1.1 copy_bitcast_fusion
  9.3 1.1 slice_bitcast_fusion.1
  10.5 1.1 slice_bitcast_fusion.5
  11.6 1.1 slice_bitcast_fusion
  12.8 1.1 slice_bitcast_fusion.4
  13.9 1.1 copy.44
  15.0 1.1 copy.45
  16.7 161.5 %while.11 = (s32[]{:T(128)}, f32[16,4,2,4096]{3,2,1,0:T(2,128)}, s32[16]{0:T(128)S(1)}, f32[3,256,64]{1,0,2:T(4,128)}, f32[3,256,1,64]{1,0,3,2:T(4,128)S(1)}, /*...) while((s32[]{:T(128)}, f32[16,4,2,4096]{3,2,1,0:T(2,128)}, ...), condition=%wide.region_1.2_spmd, body=%wide.region_0.1_spmd.sunk | while | flops 606842880 | bytes 11387647 | solution.py:69
  21.8 1.4 fusion.87
  31.9 1.4 fusion.87
  41.9 1.4 fusion.87
  52.0 1.4 fusion.87
  62.1 1.4 fusion.87
  72.2 1.4 fusion.87
  82.3 1.4 fusion.87
  92.4 1.4 fusion.87
  102.5 1.4 fusion.87
  112.6 1.4 fusion.87
  122.7 1.4 fusion.87
  132.8 1.4 fusion.87
  142.9 1.4 fusion.87
  153.0 1.4 fusion.87
  163.0 1.4 fusion.87
  173.2 1.4 fusion.87
  178.2 4.2 copy.82
  182.5 153.9 %all-gather.6.cloned.1.call-done = f32[8,64,2,4096]{3,1,2,0:T(8,128)} async-done(((f32[1,64,2,4096]{3,1,2,0:T(8,128)}), f32[8,64,2,4096]{3,1,2,0:T(8,128)}) %all-gather.6.cloned.1.call-update) | async-done | bytes 16777232 | tf_op jit(solution)/shard_map/all_gather | solution.py:12
  336.4 7.4 %reduce_sum.9 = f32[64,2,4096]{2,0,1:T(8,128)S(1)} reduce(f32[8,64,2,4096]{3,1,2,0:T(8,128)} %all-gather.6.cloned.1.call-done, f32[]{:T(128)} %constant.49.clone.1), dimensions={0}, to_apply=%region_2.3 | reduce | flops 3670016 | bytes 18874372 | tf_op jit(solution)/shard_map/reduce_sum | solution.py:12
  345.7 23.8 %all-gather.8.cloned.1.call-done = f32[32,2,4096]{2,1,0:T(2,128)} async-done(((f32[8,2,4096]{2,1,0:T(2,128)}), f32[32,2,4096]{2,1,0:T(2,128)}) %all-gather.8.cloned.1.call-update) | async-done | bytes 1048592 | tf_op jit(solution)/shard_map/all_gather | solution.py:130
  369.5 1.7 dynamic-slice_bitcast_fusion.8
  374.6 1.0 fusion.28
  376.6 1.0 fusion.5
  377.6 1.0 fusion.24
  378.7 1.0 fusion.6
  379.7 1.0 fusion.3
  380.7 1.3 copy.52
  382.1 1.6 reshape.141
  383.6 1.0 fusion.26
  384.7 1.0 fusion.4
  385.7 1.3 copy.51
  387.1 1.6 reshape.140
  388.6 11.9 %all-gather.10.cloned.1.call-done = f32[1,64,2,4096]{3,2,0,1:T(2,128)} async-done(((f32[1,8,2,4096]{3,2,0,1:T(2,128)}), f32[1,64,2,4096]{3,2,0,1:T(2,128)}) %all-gather.10.cloned.1.call-update) | async-done | bytes 2097168 | tf_op jit(solution)/shard_map/all_gather | solution.py:146
  400.5 4.6 %fusion.37 = (f32[64,1,4096]{2,1,0:T(1,128)S(1)}, f32[64,1,4096]{2,1,0:T(1,128)S(1)}) fusion(f32[64,2,4096]{2,1,0:T(2,128)} %bitcast.260), kind=kLoop, calls=%fused_computation.90 | loop fusion | bytes 4194304 | tf_op jit(solution)/shard_map/slice | solution.py:98
  405.2 1.6 fusion.11
  406.8 1.6 fusion.13
  408.4 1.6 fusion.8
  409.9 1.7 multiply_reduce_fusion.2
  411.7 15.3 %psum.7 = f32[4,2]{0,1:T(2,128)S(1)} all-reduce(f32[4,2]{0,1:T(2,128)S(1)} %pad_maximum_fusion.4), channel_id=1, replica_groups=mesh['tm'=4,'space'=8] {'space'}, use_global_device_ids=true, to_apply=%region_3.4 | all-reduce | flops 8 | bytes 64 | tf_op jit(solution)/shard_map/psum | solution.py:148
  (350 shorter events, 133.8 us)
Async XLA Ops:
  7.2 329.2 %all-gather.6.cloned.1.call-start = ((), (), s32[]{:S(2)}) async-start(), calls=%async_computation | async-start | bytes 18874368 | tf_op jit(solution)/shard_map/all_gather | solution.py:12
  182.4 187.1 %all-gather.8.cloned.1.call-start = ((), (), s32[]{:S(2)}) async-start(), calls=%async_computation.1 | async-start | bytes 1310720 | tf_op jit(solution)/shard_map/all_gather | solution.py:130
  182.5 163.2 %copy-start.5 = (s32[4,3]{1,0:T(4,128)S(1)}, s32[4,3]{1,0:T(4,128)}, u32[]{:S(2)}) copy-start(s32[4,3]{1,0:T(4,128)} %param.9) | copy-start | bytes 148
  343.7 27.5 %copy-start.3 = (f32[1,16,2,4096]{3,2,1,0:T(2,128)S(1)}, f32[1,16,2,4096]{3,2,1,0:T(2,128)}, u32[]{:S(2)}) copy-start(f32[1,16,2,4096]{3,2,1,0:T(2,128)} %param.7) | copy-start | bytes 1572868
  344.7 55.8 %all-gather.10.cloned.1.call-start = ((), (), s32[]{:S(2)}) async-start(), calls=%async_computation.2 | async-start | bytes 2359296 | tf_op jit(solution)/shard_map/all_gather | solution.py:146
  371.2 2.5 copy-start
  372.4 5.2 %copy-start.1 = (f32[4,64,64,1]{2,1,0,3:T(8,128)}, f32[4,64,64,1]{2,1,0,3:T(8,128)S(1)}, u32[]{:S(2)}) copy-start(f32[4,64,64,1]{2,1,0,3:T(8,128)S(1)} %reshape.152) | copy-start | bytes 196612
  380.7 2.9 copy-start.2
  405.2 4.7 %copy-start.4 = (f32[4,8,64]{2,1,0:T(8,128)S(1)}, f32[4,8,64]{2,1,0:T(8,128)}, u32[]{:S(2)}) copy-start(f32[4,8,64]{2,1,0:T(8,128)} %copy.69) | copy-start | bytes 24580
Sparse Core Ops, SparseCore 0:
  182.5 153.7 all-gather.5
  344.8 24.6 all-gather.7
  371.4 29.1 all-gather.9
